TPU v7x, 256 devices: a whole 4x4x8 slice. The times are simulated.
256 devices in a mesh: seq: 32 (over z_lo, y, core), batch: 8 (over x, z_hi).
Axes of the slice: x: 4, y: 4, z: 8 (z_hi: 2, z_lo: 4; z = z_hi * 4 + z_lo), core: 2. Of those that a mesh axis runs over, the one named last changes fastest.
Arguments:
- coarse: bfloat16 [8, 8192, 1536], P('batch', 'seq'), may hold values from -6 to 6
- skip: bfloat16 [8, 16384, 1536], P('batch', 'seq'), may hold values from -6 to 6
- depth_kernel: float32 [3, 1536], replicated, may hold values from -3.5 to 3.5
- sep_weight: bfloat16 [1536, 1536], P('seq'), may hold values from -0.15625 to 0.15625
- sep_bias: float32 [1536], replicated, may hold values from -3 to 3
- head_weight: bfloat16 [1536, 3840], P(None, 'seq'), may hold values from -0.15625 to 0.15625
- head_bias: float32 [3840], replicated, may hold values from -4 to 4
- strand_pair: int32 [3840], replicated, may hold values from 0 to 3839, as said below
Outputs:
- preds: bfloat16 [8, 16384, 3840], P('batch', 'seq')
Inputs may be any that keep to these rules, and one draw needn't show every extreme that they name: strand_pair is a permutation with strand_pair[strand_pair[t]] == t; about half of the tracks are paired with another one.
All inputs are finite; a program needn't handle non-finite values.
Results may differ from a plain program's by a relative error of at most 0.0053.
Values may be sent and summed in bfloat16 or wider, within the bound.
A program may use at most 64 MiB of HBM per device.

v0:
```python
import jax
import jax.numpy as jnp
from jax import lax
from jax.sharding import PartitionSpec as P


def with_halo(cells, axis, width):
    count = lax.axis_size(axis)
    ends = count - 1
    head = lax.slice_in_dim(cells, 0, width, axis=0)
    tail = lax.slice_in_dim(cells, cells.shape[0] - width, cells.shape[0], axis=0)
    return jnp.concatenate(
        [
            lax.ppermute(tail, axis, [(i, (i + 1) % count) for i in range(ends)]),
            cells,
            lax.ppermute(head, axis, [((i + 1) % count, i) for i in range(ends)]),
        ],
        axis=0,
    )


def reversed_rows(x):
    rows = x.shape[0]
    r = lax.broadcasted_iota(jnp.int32, (rows, rows), 0)
    c = lax.broadcasted_iota(jnp.int32, (rows, rows), 1)
    flip = (r + c == rows - 1).astype(x.dtype)
    return jnp.dot(flip, x, preferred_element_type=jnp.float32).astype(x.dtype)


def to_mirror(x):
    nb, ns = (lax.axis_size("batch"), lax.axis_size("seq"))
    half = nb // 2
    route = []
    for s in range(ns):
        for b in range(nb):
            mirror = (ns - 1 - s) * nb + (b + half) % nb
            route.append((s * nb + b, mirror))
    return lax.ppermute(x, ("seq", "batch"), route)


def per_device(
    coarse, skip, depth_kernel, sep_weight, sep_bias, head_weight, head_bias, strand_pair
):
    sep_full = lax.all_gather(sep_weight, "seq", axis=0, tiled=True)
    head_full = lax.all_gather(head_weight, "seq", axis=1, tiled=True)
    upsampled = jnp.repeat(coarse[0].astype(jnp.float32), 2, axis=0)
    merged = (upsampled + skip[0]).astype(jnp.bfloat16)
    padded = with_halo(merged, "seq", 1)
    depthwise = (
        depth_kernel[0] * padded[:-2]
        + depth_kernel[1] * padded[1:-1]
        + depth_kernel[2] * padded[2:]
    )
    depthwise = depthwise.astype(jnp.bfloat16)
    mirrored = to_mirror(reversed_rows(depthwise))

    def head(block):
        pointwise = jnp.dot(block, sep_full, preferred_element_type=jnp.float32)
        features = jax.nn.gelu(pointwise + sep_bias, approximate=True).astype(jnp.bfloat16)
        logits = jnp.dot(features, head_full, preferred_element_type=jnp.float32)
        return jax.nn.softplus(logits + head_bias).astype(jnp.bfloat16)

    own = head(depthwise)
    other = jnp.take(head(mirrored), strand_pair, axis=1)
    averaged = 0.5 * (own.astype(jnp.float32) + other.astype(jnp.float32))
    return averaged.astype(jnp.bfloat16)[None]


def solution(mesh):
    in_specs = (
        P("batch", "seq", None),
        P("batch", "seq", None),
        P(),
        P("seq", None),
        P(),
        P(None, "seq"),
        P(),
        P(),
    )
    return jax.shard_map(
        per_device, mesh=mesh, in_specs=in_specs, out_specs=P("batch", "seq", None), check_vma=False
    )
```

profile of v0, /device:TPU:1, one launch (start us, length us, event | category | flops | bytes accessed | tf_op | source)
XLA Modules:
  0.0 285.9 jit_solution(13165414521046507312)
XLA Ops:
  6.5 0.0 all-gather.3.cloned.1.call-start
  6.5 0.7 all-gather.3.cloned.1.call-update
  7.3 0.0 all-gather.5.cloned.1.call-start
  7.3 0.7 all-gather.5.cloned.1.call-update
  8.0 1.3 bitcast_convert_fusion
  9.3 1.1 broadcast_in_dim.22
  10.4 3.3 %reshape.14 = f32[512,1536]{1,0:T(8,128)} reshape(f32[256,2,1536]{2,1,0:T(2,128)S(1)} %broadcast_in_dim.22) | data formatting | bytes 6291456 | tf_op jit(solution)/shard_map/reshape | solution.py:46
  13.7 0.0 copy-start.1
  13.7 2.8 fusion.19
  16.6 4.6 %collective-permute-start = (bf16[1,1536]{1,0:T(2,128)(2,1)S(1)}, bf16[1,1536]{1,0:T(2,128)(2,1)S(1)}, u32[]{:S(2)}, u32[]{:S(2)}) collective-permute-start(bf16[1,1536]{1,0:T(2,128)(2,1)S(1)} %get-tuple-element.8), channel_id=1, source_target_pairs={{0,8},{8,16},{16,24},{24,32},{32,40},{40,48},{48,56},{56,64},{64,7... | collective-permute-start | bytes 9224 | tf_op jit(solution)/shard_map/ppermute | solution.py:14
  21.2 1.9 collective-permute-start.1
  23.1 0.0 copy-done.1
  23.1 0.1 slice_reduce_fusion.2
  23.2 0.0 collective-permute-done
  23.2 2.9 %collective-permute-done.1 = bf16[1,1536]{1,0:T(2,128)(2,1)S(1)} collective-permute-done((bf16[1,1536]{1,0:T(2,128)(2,1)S(1)}, bf16[1,1536]{1,0:T(2,128)(2,1)S(1)}, u32[]{:S(2)}, u32[]{:S(2)}) %collective-permute-start.1) | collective-permute-done | bytes 3104 | tf_op jit(solution)/shard_map/ppermute | solution.py:16
  26.1 0.0 copy-start
  26.1 0.0 copy-start.3
  26.1 1.5 convolution_convert_fusion
  27.7 8.3 %collective-permute-start.2 = (bf16[512,1536]{1,0:T(8,128)(2,1)S(1)}, bf16[512,1536]{1,0:T(8,128)(2,1)S(1)}, u32[]{:S(2)}, u32[]{:S(2)}) collective-permute-start(bf16[512,1536]{1,0:T(8,128)(2,1)S(1)} %convolution_convert_fusion), channel_id=1, source_target_pairs={{0,252},{1,253},{2,254},{3,255},{4,248},{5,249},{6,250},{7,251},{8... | collective-permute-start | bytes 4718600 | tf_op jit(solution)/shard_map/ppermute | solution.py:38
  35.9 0.0 copy-done
  36.0 0.0 copy-start.2
  36.0 39.6 %collective-permute-done.2 = bf16[512,1536]{1,0:T(8,128)(2,1)S(1)} collective-permute-done((bf16[512,1536]{1,0:T(8,128)(2,1)S(1)}, bf16[512,1536]{1,0:T(8,128)(2,1)S(1)}, u32[]{:S(2)}, u32[]{:S(2)}) %collective-permute-start.2) | collective-permute-done | bytes 1572896 | tf_op jit(solution)/shard_map/ppermute | solution.py:38
  75.6 64.0 %all-gather.3.cloned.1.call-done = bf16[1536,1536]{1,0:T(8,128)(2,1)} async-done(((bf16[48,1536]{1,0:T(8,128)(2,1)}), bf16[1536,1536]{1,0:T(8,128)(2,1)}) %all-gather.3.cloned.1.call-update) | async-done | bytes 4718608 | tf_op jit(solution)/shard_map/all_gather | solution.py:44
  139.6 0.0 copy-done.3
  139.6 6.6 %fusion.20 = bf16[512,1536]{1,0:T(8,128)(2,1)} fusion(bf16[512,1536]{1,0:T(8,128)(2,1)S(1)} %collective-permute-done.2, bf16[1536,1536]{1,0:T(8,128)(2,1)} %all-gather.3.cloned.1.call-done, f32[1536]{0:T(1024)S(1)} %copy-done.3), kind=kOutput, calls=%fused_computation.31 | convolution fusion | flops 2423783424 | bytes 7870464 | tf_op jit(solution)/shard_map/dot_general | solution.py:58
  146.2 70.0 %all-gather.5.cloned.1.call-done = bf16[1536,3840]{0,1:T(8,128)(2,1)} async-done(((bf16[1536,120]{0,1:T(8,128)(2,1)}), bf16[1536,3840]{0,1:T(8,128)(2,1)}) %all-gather.5.cloned.1.call-update) | async-done | bytes 11796496 | tf_op jit(solution)/shard_map/all_gather | solution.py:45
  216.2 0.0 copy-done.2
  216.2 15.1 %fusion.1 = bf16[512,3840]{1,0:T(8,128)(2,1)} fusion(bf16[512,1536]{1,0:T(8,128)(2,1)} %fusion.20, bf16[1536,3840]{0,1:T(8,128)(2,1)} %all-gather.5.cloned.1.call-done, f32[3840]{0:T(1024)S(1)} %copy-done.2), kind=kOutput, calls=%fused_computation.4 | convolution fusion | flops 6055526400 | bytes 17316864 | tf_op jit(solution)/shard_map/dot_general | solution.py:60
  231.4 6.3 %copy.9 = bf16[512,3840]{0,1:T(8,128)(2,1)} copy(bf16[512,3840]{1,0:T(8,128)(2,1)} %fusion.1) | data formatting | bytes 7864320 | tf_op jit(solution)/shard_map/convert_element_type | solution.py:61
  237.6 14.5 %gather_fusion = bf16[3840,512]{1,0:T(8,128)(2,1)} fusion(bf16[512,3840]{0,1:T(8,128)(2,1)} %copy.9, s32[4096]{0:T(1024)S(1)} %pad_clamp_fusion), kind=kCustom, calls=%fused_computation | custom fusion | bytes 7879680 | tf_op jit(solution)/shard_map/jit(_take)/gather | solution.py:64
  252.1 6.3 %copy.10 = bf16[3840,512]{0,1:T(8,128)(2,1)} copy(bf16[3840,512]{1,0:T(8,128)(2,1)} %gather_fusion) | data formatting | bytes 7864320 | tf_op jit(solution)/shard_map/jit(_take)/gather | solution.py:64
  258.4 20.7 %fusion.4 = bf16[1,512,3840]{2,1,0:T(8,128)(2,1)} fusion(bf16[1536,3840]{0,1:T(8,128)(2,1)} %all-gather.5.cloned.1.call-done, bf16[3840,512]{0,1:T(8,128)(2,1)} %copy.10, f32[3840]{0:T(1024)S(1)} %copy-done.2, pred[3840]{0:T(1024)(128)(4,1)S(1)} %compare_and_fusion, bf16[1536,1536]{1,0:T(8,128)(2,1)} %all-gather.3.cloned.1.call-done, ...), kind=kOutput, calls=%fused_computation.8 | convolution fusion | flops 8502902784 | bytes 26002176 | tf_op jit(solution)/shard_map/dot_general | solution.py:60
  (4 shorter events, 0.0 us)
Async XLA Ops:
  6.5 133.1 %all-gather.3.cloned.1.call-start = ((), (), s32[]{:S(2)}) async-start(), calls=%async_computation | async-start | bytes 4866048 | tf_op jit(solution)/shard_map/all_gather | solution.py:44
  7.3 209.0 %all-gather.5.cloned.1.call-start = ((), (), s32[]{:S(2)}) async-start(), calls=%async_computation.1 | async-start | bytes 12165120 | tf_op jit(solution)/shard_map/all_gather | solution.py:45
  13.7 9.4 %copy-start.1 = (f32[3,1536]{1,0:T(4,128)S(1)}, f32[3,1536]{1,0:T(4,128)}, u32[]{:S(2)}) copy-start(f32[3,1536]{1,0:T(4,128)} %param.10) | copy-start | bytes 55300
  16.6 6.6 %collective-permute-start = (bf16[1,1536]{1,0:T(2,128)(2,1)S(1)}, bf16[1,1536]{1,0:T(2,128)(2,1)S(1)}, u32[]{:S(2)}, u32[]{:S(2)}) collective-permute-start(bf16[1,1536]{1,0:T(2,128)(2,1)S(1)} %get-tuple-element.8), channel_id=1, source_target_pairs={{0,8},{8,16},{16,24},{24,32},{32,40},{40,48},{48,56},{56,64},{64,7... | collective-permute-start | bytes 9224 | tf_op jit(solution)/shard_map/ppermute | solution.py:14
  21.2 4.9 %collective-permute-start.1 = (bf16[1,1536]{1,0:T(2,128)(2,1)S(1)}, bf16[1,1536]{1,0:T(2,128)(2,1)S(1)}, u32[]{:S(2)}, u32[]{:S(2)}) collective-permute-start(bf16[1,1536]{1,0:T(2,128)(2,1)S(1)} %get-tuple-element.9), channel_id=1, source_target_pairs={{8,0},{16,8},{24,16},{32,24},{40,32},{48,40},{56,48},{64,56},{72,6... | collective-permute-start | bytes 9224 | tf_op jit(solution)/shard_map/ppermute | solution.py:16
  26.1 9.8 %copy-start = (s32[3840]{0:T(1024)S(1)}, s32[3840]{0:T(1024)}, u32[]{:S(2)}) copy-start(s32[3840]{0:T(1024)} %param.15) | copy-start | bytes 46084
  26.1 113.5 %copy-start.3 = (f32[1536]{0:T(1024)S(1)}, f32[1536]{0:T(1024)}, u32[]{:S(2)}) copy-start(f32[1536]{0:T(1024)} %param.12) | copy-start | bytes 18436
  27.7 48.0 %collective-permute-start.2 = (bf16[512,1536]{1,0:T(8,128)(2,1)S(1)}, bf16[512,1536]{1,0:T(8,128)(2,1)S(1)}, u32[]{:S(2)}, u32[]{:S(2)}) collective-permute-start(bf16[512,1536]{1,0:T(8,128)(2,1)S(1)} %convolution_convert_fusion), channel_id=1, source_target_pairs={{0,252},{1,253},{2,254},{3,255},{4,248},{5,249},{6,250},{7,251},{8... | collective-permute-start | bytes 4718600 | tf_op jit(solution)/shard_map/ppermute | solution.py:38
  36.0 180.3 %copy-start.2 = (f32[3840]{0:T(1024)S(1)}, f32[3840]{0:T(1024)}, u32[]{:S(2)}) copy-start(f32[3840]{0:T(1024)} %param.14) | copy-start | bytes 46084
Sparse Core Ops, SparseCore 0:
  9.2 130.4 all-gather.2
  141.5 74.6 all-gather.4
where the time goes:
time: 286 us
  waiting for transfers between devices  178 us (62%)
  matrix products  44 us (15%)
  local copies, waits for them, and re-layouts  31.5 us (11%)
  starting transfers between devices  14.8 us (5%)
  between operations  13.5 us (5%)
  other arithmetic  4.14 us (1%)
    all_gather x1, waiting for transfers between devices, per_device(): head_full = lax.all_gather(head_weight, 'seq', axis=1, tiled=True)  70 us
    all_gather x1, waiting for transfers between devices, per_device(): sep_full = lax.all_gather(sep_weight, 'seq', axis=0, tiled=True)  64 us
    ppermute x1, waiting for transfers between devices, to_mirror(): return lax.ppermute(x, ('seq', 'batch'), route)  39.6 us
    dot_general x2, matrix products, head(): logits = jnp.dot(features, head_full, preferred_element_type=jnp.float32)  35.8 us
    gather x2, local copies, waits for them, and re-layouts, per_device(): other = jnp.take(head(mirrored), strand_pair, axis=1)  20.7 us
    ppermute x1, starting transfers between devices, to_mirror(): return lax.ppermute(x, ('seq', 'batch'), route)  8.27 us
    dot_general x1, matrix products, head(): pointwise = jnp.dot(block, sep_full, preferred_element_type=jnp.float32)  6.6 us
    convert_element_type x1, local copies, waits for them, and re-layouts, head(): return jax.nn.softplus(logits + head_bias).astype(jnp.bfloat16)  6.29 us
  transfers between devices with their start and end apart: 5, of which 4 were waited for; matrix products, arithmetic and copies ran while one was open for 6% of the time, Pallas kernels for 0%

commit v1 on v0

--- a/solution.py
+++ b/solution.py
@@ -2,6 +2,12 @@
 import jax.numpy as jnp
 from jax import lax
 from jax.sharding import PartitionSpec as P
+
+
+def bars_change(u):
+    r2 = jnp.stack([u for _ in range(lax.axis_size("seq"))], axis=0)
+    arr_out = lax.all_to_all(r2, "seq", 0, 0)
+    return jnp.concatenate(arr_out, 1)
 
 
 def with_halo(cells, axis, width):
@@ -42,7 +48,7 @@
     coarse, skip, depth_kernel, sep_weight, sep_bias, head_weight, head_bias, strand_pair
 ):
     sep_full = lax.all_gather(sep_weight, "seq", axis=0, tiled=True)
-    head_full = lax.all_gather(head_weight, "seq", axis=1, tiled=True)
+    head_full = bars_change(head_weight)
     upsampled = jnp.repeat(coarse[0].astype(jnp.float32), 2, axis=0)
     merged = (upsampled + skip[0]).astype(jnp.bfloat16)
     padded = with_halo(merged, "seq", 1)

time: 286 us -> 453 us (1.58)
  the two profiles are of different devices: /device:TPU:1 before, /device:TPU:57 now
where the time goes in v1:
time: 453 us; the launch traced here: 452 us
  waiting for transfers between devices  335 us (74%)
  matrix products  44 us (10%)
  local copies, waits for them, and re-layouts  37.5 us (8%)
  starting transfers between devices  19.5 us (4%)
  between operations  13.5 us (3%)
    ppermute x1, waiting for transfers between devices, with_halo(): lax.ppermute(head, axis, [((i + 1) % count, i) for i in range(ends)])  303 us
    dot_general x2, matrix products, head(): logits = jnp.dot(features, head_full, preferred_element_type=jnp.float32)  35.8 us
    ppermute x1, waiting for transfers between devices, to_mirror(): return lax.ppermute(x, ('seq', 'batch'), route)  31.4 us
    gather x2, local copies, waits for them, and re-layouts, per_device(): other = jnp.take(head(mirrored), strand_pair, axis=1)  20.7 us
  transfers between devices with their start and end apart: 5, of which 2 were waited for; matrix products, arithmetic and copies ran while one was open for 3% of the time, Pallas kernels for 0%

profile of v1, /device:TPU:57, one launch (start us, length us, event | category | flops | bytes accessed | tf_op | source)
XLA Modules:
  0.0 452.4 jit_solution(5771915756916947681)
XLA Ops:
  6.5 6.0 %stack.2 = bf16[32,1536,120]{1,2,0:T(8,128)(2,1)} broadcast(bf16[1536,120]{0,1:T(8,128)(2,1)} %param.13), dimensions={1,2} | broadcast | bytes 12165120 | tf_op jit(solution)/shard_map/stack | solution.py:8
  12.5 0.0 copy-start
  12.6 8.9 %all-to-all-start = ((bf16[32,1536,120]{1,2,0:T(8,128)(2,1)}), bf16[32,1536,120]{1,2,0:T(8,128)(2,1)}, u32[]{:S(2)}, u32[]{:S(2)}) async-start(bf16[32,1536,120]{1,2,0:T(8,128)(2,1)} %stack.2), calls=%async_computation | async-start | bytes 23592960 | tf_op jit(solution)/shard_map/all_to_all | solution.py:9
  21.5 0.0 all-gather.2.cloned.1.call-start
  21.5 0.7 all-gather.2.cloned.1.call-update
  22.2 0.0 copy-done
  22.2 0.2 bitcast_convert_fusion
  22.4 1.1 broadcast_in_dim.22
  23.5 3.3 reshape.22
  26.8 0.0 copy-start.2
  26.8 2.8 fusion.19
  29.7 2.3 collective-permute-start.1
  32.0 5.4 %collective-permute-start = (bf16[1,1536]{1,0:T(2,128)(2,1)S(1)}, bf16[1,1536]{1,0:T(2,128)(2,1)S(1)}, u32[]{:S(2)}, u32[]{:S(2)}) collective-permute-start(bf16[1,1536]{1,0:T(2,128)(2,1)S(1)} %get-tuple-element.8), channel_id=1, source_target_pairs={{0,8},{8,16},{16,24},{24,32},{32,40},{40,48},{48,56},{56,64},{64,7... | collective-permute-start | bytes 9224 | tf_op jit(solution)/shard_map/ppermute | solution.py:20
  37.4 0.0 copy-done.2
  37.4 0.1 slice_reduce_fusion.2
  37.4 302.9 %collective-permute-done.1 = bf16[1,1536]{1,0:T(2,128)(2,1)S(1)} collective-permute-done((bf16[1,1536]{1,0:T(2,128)(2,1)S(1)}, bf16[1,1536]{1,0:T(2,128)(2,1)S(1)}, u32[]{:S(2)}, u32[]{:S(2)}) %collective-permute-start.1) | collective-permute-done | bytes 3104 | tf_op jit(solution)/shard_map/ppermute | solution.py:22
  340.3 0.0 collective-permute-done
  340.3 0.0 copy-start.1
  340.3 0.0 copy-start.4
  340.3 1.5 convolution_convert_fusion
  341.9 2.9 collective-permute-start.2
  344.7 0.0 copy-done.1
  344.8 0.0 copy-start.3
  344.8 31.4 %collective-permute-done.2 = bf16[512,1536]{1,0:T(8,128)(2,1)S(1)} collective-permute-done((bf16[512,1536]{1,0:T(8,128)(2,1)S(1)}, bf16[512,1536]{1,0:T(8,128)(2,1)S(1)}, u32[]{:S(2)}, u32[]{:S(2)}) %collective-permute-start.2) | collective-permute-done | bytes 1572896 | tf_op jit(solution)/shard_map/ppermute | solution.py:44
  376.1 0.0 all-gather.2.cloned.1.call-done
  376.1 0.0 copy-done.4
  376.2 6.6 %fusion.20 = bf16[512,1536]{1,0:T(8,128)(2,1)} fusion(bf16[512,1536]{1,0:T(8,128)(2,1)S(1)} %collective-permute-done.2, bf16[1536,1536]{1,0:T(8,128)(2,1)} %all-gather.2.cloned.1.call-done, f32[1536]{0:T(1024)S(1)} %copy-done.4), kind=kOutput, calls=%fused_computation.31 | convolution fusion | flops 2423783424 | bytes 7870464 | tf_op jit(solution)/shard_map/dot_general | solution.py:64
  382.8 0.0 all-to-all-done
  382.8 0.0 copy-done.3
  382.8 15.1 %fusion.1 = bf16[512,3840]{1,0:T(8,128)(2,1)} fusion(bf16[512,1536]{1,0:T(8,128)(2,1)} %fusion.20, bf16[1536,3840]{0,1:T(8,128)(2,1)} %bitcast.3, f32[3840]{0:T(1024)S(1)} %copy-done.3), kind=kOutput, calls=%fused_computation.4 | convolution fusion | flops 6055526400 | bytes 17316864 | tf_op jit(solution)/shard_map/dot_general | solution.py:66
  397.9 6.3 %copy.12 = bf16[512,3840]{0,1:T(8,128)(2,1)} copy(bf16[512,3840]{1,0:T(8,128)(2,1)} %fusion.1) | data formatting | bytes 7864320 | tf_op jit(solution)/shard_map/convert_element_type | solution.py:67
  404.2 14.5 %gather_fusion = bf16[3840,512]{1,0:T(8,128)(2,1)} fusion(bf16[512,3840]{0,1:T(8,128)(2,1)} %copy.12, s32[4096]{0:T(1024)S(1)} %pad_clamp_fusion), kind=kCustom, calls=%fused_computation | custom fusion | bytes 7879680 | tf_op jit(solution)/shard_map/jit(_take)/gather | solution.py:70
  418.7 6.2 %copy.13 = bf16[3840,512]{0,1:T(8,128)(2,1)} copy(bf16[3840,512]{1,0:T(8,128)(2,1)} %gather_fusion) | data formatting | bytes 7864320 | tf_op jit(solution)/shard_map/jit(_take)/gather | solution.py:70
  424.9 20.7 %fusion.4 = bf16[1,512,3840]{2,1,0:T(8,128)(2,1)} fusion(bf16[1536,3840]{0,1:T(8,128)(2,1)} %bitcast.3, bf16[3840,512]{0,1:T(8,128)(2,1)} %copy.13, f32[3840]{0:T(1024)S(1)} %copy-done.3, pred[3840]{0:T(1024)(128)(4,1)S(1)} %compare_and_fusion, bf16[1536,1536]{1,0:T(8,128)(2,1)} %all-gather.2.cloned.1.call-done, f32[1536]{0:T(1024)S(1)} %copy-done.4, ...), kind=kOutput, calls=%fused_computation.8 | convolution fusion | flops 8502902784 | bytes 26002176 | tf_op jit(solution)/shard_map/dot_general | solution.py:66
  (4 shorter events, 0.0 us)
Async XLA Ops:
  12.5 9.7 %copy-start = (bf16[1,256,1536]{2,1,0:T(8,128)(2,1)S(1)}, bf16[1,256,1536]{2,1,0:T(8,128)(2,1)}, u32[]{:S(2)}) copy-start(bf16[1,256,1536]{2,1,0:T(8,128)(2,1)} %param.8) | copy-start | bytes 2359300
  12.6 370.2 %all-to-all-start = ((bf16[32,1536,120]{1,2,0:T(8,128)(2,1)}), bf16[32,1536,120]{1,2,0:T(8,128)(2,1)}, u32[]{:S(2)}, u32[]{:S(2)}) async-start(bf16[32,1536,120]{1,2,0:T(8,128)(2,1)} %stack.2), calls=%async_computation | async-start | bytes 23592960 | tf_op jit(solution)/shard_map/all_to_all | solution.py:9
  21.5 354.7 %all-gather.2.cloned.1.call-start = ((), (), s32[]{:S(2)}) async-start(), calls=%async_computation.1 | async-start | bytes 4866048 | tf_op jit(solution)/shard_map/all_gather | solution.py:50
  26.8 10.5 %copy-start.2 = (f32[3,1536]{1,0:T(4,128)S(1)}, f32[3,1536]{1,0:T(4,128)}, u32[]{:S(2)}) copy-start(f32[3,1536]{1,0:T(4,128)} %param.10) | copy-start | bytes 55300
  29.7 310.7 %collective-permute-start.1 = (bf16[1,1536]{1,0:T(2,128)(2,1)S(1)}, bf16[1,1536]{1,0:T(2,128)(2,1)S(1)}, u32[]{:S(2)}, u32[]{:S(2)}) collective-permute-start(bf16[1,1536]{1,0:T(2,128)(2,1)S(1)} %get-tuple-element.9), channel_id=1, source_target_pairs={{8,0},{16,8},{24,16},{32,24},{40,32},{48,40},{56,48},{64,56},{72,6... | collective-permute-start | bytes 9224 | tf_op jit(solution)/shard_map/ppermute | solution.py:22
  32.0 308.3 %collective-permute-start = (bf16[1,1536]{1,0:T(2,128)(2,1)S(1)}, bf16[1,1536]{1,0:T(2,128)(2,1)S(1)}, u32[]{:S(2)}, u32[]{:S(2)}) collective-permute-start(bf16[1,1536]{1,0:T(2,128)(2,1)S(1)} %get-tuple-element.8), channel_id=1, source_target_pairs={{0,8},{8,16},{16,24},{24,32},{32,40},{40,48},{48,56},{56,64},{64,7... | collective-permute-start | bytes 9224 | tf_op jit(solution)/shard_map/ppermute | solution.py:20
  340.3 4.4 copy-start.1
  340.3 35.8 %copy-start.4 = (f32[1536]{0:T(1024)S(1)}, f32[1536]{0:T(1024)}, u32[]{:S(2)}) copy-start(f32[1536]{0:T(1024)} %param.12) | copy-start | bytes 18436
  341.9 34.3 %collective-permute-start.2 = (bf16[512,1536]{1,0:T(8,128)(2,1)S(1)}, bf16[512,1536]{1,0:T(8,128)(2,1)S(1)}, u32[]{:S(2)}, u32[]{:S(2)}) collective-permute-start(bf16[512,1536]{1,0:T(8,128)(2,1)S(1)} %convolution_convert_fusion), channel_id=1, source_target_pairs={{0,252},{1,253},{2,254},{3,255},{4,248},{5,249},{6,250},{7,251},{8... | collective-permute-start | bytes 4718600 | tf_op jit(solution)/shard_map/ppermute | solution.py:44
  344.8 38.0 %copy-start.3 = (f32[3840]{0:T(1024)S(1)}, f32[3840]{0:T(1024)}, u32[]{:S(2)}) copy-start(f32[3840]{0:T(1024)} %param.14) | copy-start | bytes 46084
Sparse Core Ops, SparseCore 0:
  24.1 167.7 all-gather.1
